TPU v7x, 256 devices: a whole 4x4x8 slice. The times are simulated.
256 devices in a mesh: dp: 8 (over y, x_hi), mp: 32 (over z, x_lo, core).
Axes of the slice: x: 4 (x_hi: 2, x_lo: 2; x = x_hi * 2 + x_lo), y: 4, z: 8, core: 2. Of those that a mesh axis runs over, the one named last changes fastest.
Arguments:
- activations: bfloat16 [4096, 4096], P('dp', 'mp'), may hold values from -22 to 22
- out_grads: bfloat16 [4096, 32768], P('dp', 'mp'), may hold values from -1 to 1
- weight: float32 [4096, 32768], P('dp', 'mp'), may hold values from -0.09375 to 0.09375
- row_state: float32 [4096], P('dp'), may hold values from 0.1 to 1.6
- column_state: float32 [32768], P('mp'), may hold values from 0.1 to 1.6
- next_batch: bfloat16 [4096, 4096], P('dp', 'mp'), may hold values from -6 to 6
Outputs:
- new_weight: float32 [4096, 32768], P('dp', 'mp')
- update: float32 [4096, 32768], P('dp', 'mp')
- row_moment: float32 [4096], P('dp')
- column_moment: float32 [32768], P('mp')
- next_hidden: bfloat16 [4096, 32768], P('dp', 'mp')
All inputs are finite; a program needn't handle non-finite values.
Results may differ from a plain program's by a relative error of at most 0.001.
The roundings to bfloat16 on the way count: a program that leaves them out, or rounds other values in their place, can miss the bound.
Values may be sent and summed in bfloat16 or wider, within the bound.
A program may use at most 128 MiB of HBM per device.

v0:
```python
import jax
import jax.numpy as jnp
from jax import lax
from jax.sharding import PartitionSpec as P

D = 4096
FF = 32768
tiny_square = 1e-30
weight_eps = 1e-06
decay_rate = 0.5
clip_level = 0.5
learn_rate = 0.01


def body(activations, out_grads, weight, row_state, column_state, next_batch):
    features, next_features = (
        lax.all_gather(activations, "mp", axis=1, tiled=True),
        lax.all_gather(next_batch, "mp", axis=1, tiled=True),
    )
    contract = (((0,), (0,)), ((), ()))
    block = features
    gradient = lax.psum_scatter(
        lax.dot_general(block, out_grads, contract, preferred_element_type=jnp.float32),
        "dp",
        scatter_dimension=0,
        tiled=True,
    )
    squares = gradient * gradient + tiny_square
    row_part = jnp.sum(squares, axis=1)
    column_part = jnp.sum(squares, axis=0)
    row_sum = lax.psum(row_part, "mp")
    column_sum = lax.psum(column_part, "dp")
    row_moment = decay_rate * row_state + (1.0 - decay_rate) * (row_sum / FF)
    column_moment = decay_rate * column_state + (1.0 - decay_rate) * (column_sum / D)
    raw_update = gradient * lax.rsqrt(row_moment[:, None] * column_moment[None, :])
    raw_total, weight_total = lax.psum(
        (jnp.sum(raw_update * raw_update), jnp.sum(weight * weight)), ("dp", "mp")
    )
    rms_update = jnp.sqrt(raw_total / (D * FF))
    update = raw_update / jnp.maximum(1.0, rms_update / clip_level)
    rms_weight = jnp.sqrt(weight_total / (D * FF) + weight_eps)
    new_weight = weight - learn_rate * rms_weight * update
    weight_half = new_weight.astype(jnp.bfloat16)
    block = next_features
    hidden_sum = jnp.dot(
        block,
        lax.all_gather(weight_half, "dp", axis=0, tiled=True),
        preferred_element_type=jnp.float32,
    )
    return (new_weight, update, row_moment, column_moment, hidden_sum.astype(jnp.bfloat16))


def solution(mesh):
    return jax.shard_map(
        body,
        mesh=mesh,
        in_specs=(P("dp", "mp"), P("dp", "mp"), P("dp", "mp"), P("dp"), P("mp"), P("dp", "mp")),
        out_specs=(P("dp", "mp"), P("dp", "mp"), P("dp"), P("mp"), P("dp", "mp")),
        check_vma=False,
    )
```

profile of v0, /device:TPU:1, one launch (start us, length us, event | category | flops | bytes accessed | tf_op | source)
XLA Modules:
  0.0 577.7 jit_solution(11072777842069617354)
XLA Ops:
  7.2 0.0 copy-start
  7.2 0.0 all-gather.4.cloned.1.call-start
  7.2 0.7 all-gather.4.cloned.1.call-update
  7.9 0.0 reduce-scatter.2.cloned.1.call-start
  8.0 78.1 %all-gather.4.cloned.1.call-done = bf16[512,4096]{1,0:T(8,128)(2,1)} async-done(((bf16[512,128]{1,0:T(8,128)(2,1)}), bf16[512,4096]{1,0:T(8,128)(2,1)}) %all-gather.4.cloned.1.call-update) | async-done | bytes 4194320 | tf_op jit(solution)/shard_map/all_gather | solution.py:17
  86.1 10.4 %fusion.6 = f32[4096,1024]{1,0:T(8,128)} fusion(bf16[512,4096]{1,0:T(8,128)(2,1)} %all-gather.4.cloned.1.call-done, bf16[512,1024]{1,0:T(8,128)(2,1)S(1)} %copy-done), kind=kOutput, calls=%fused_computation.13 | convolution fusion | flops 4294967296 | bytes 22020096 | tf_op jit(solution)/shard_map/dot_general | solution.py:23
  96.5 0.0 reduce-scatter.2.cloned.1.call-update
  96.5 0.0 all-gather.8.cloned.1.call-start
  96.5 0.7 all-gather.8.cloned.1.call-update
  97.3 0.0 all-gather.6.cloned.1.call-start
  97.3 0.8 copy-done.2
  98.1 1.1 multiply_reduce_fusion.1
  99.2 191.7 %reduce-scatter.2.cloned.1.call-done = f32[512,1024]{1,0:T(8,128)} async-done(((f32[4096,1024]{1,0:T(8,128)}), f32[512,1024]{1,0:T(8,128)}) %reduce-scatter.2.cloned.1.call-update) | async-done | bytes 2097168 | tf_op jit(solution)/shard_map/reduce_scatter | solution.py:22
  290.9 2.1 fusion.1
  293.1 56.9 %psum.29 = f32[512]{0:T(512)S(1)} all-reduce(f32[512]{0:T(512)S(1)} %get-tuple-element.10), channel_id=1, replica_groups=mesh['dp'=8,'mp'=32] {'mp'}, use_global_device_ids=true, to_apply=%region_4.0 | all-reduce | flops 512 | bytes 4096 | tf_op jit(solution)/shard_map/psum | solution.py:31
  350.0 18.5 %psum.30 = f32[1024]{0:T(1024)S(1)} all-reduce(f32[1024]{0:T(1024)S(1)} %get-tuple-element.11), channel_id=1, replica_groups=mesh['dp'=8,'mp'=32] {'dp'}, use_global_device_ids=true, to_apply=%region_6.0 | all-reduce | flops 1024 | bytes 8192 | tf_op jit(solution)/shard_map/psum | solution.py:32
  368.5 1.5 multiply_reduce_fusion
  370.0 76.3 %all-reduce = (f32[]{:T(128)}, f32[]{:T(128)}) all-reduce(f32[]{:T(128)} %multiply_reduce_fusion, f32[]{:T(128)} %multiply_reduce_fusion.1), channel_id=1, replica_groups=mesh['dp'=8,'mp'=32] {'dp','mp'}, use_global_device_ids=true, to_apply=%region_8.0 | all-reduce | flops 2 | bytes 16 | tf_op jit(solution)/shard_map/psum | solution.py:36
  447.7 4.5 fusion.4
  452.2 0.0 all-gather.6.cloned.1.call-update
  452.3 0.0 all-gather.8.cloned.1.call-done
  452.3 108.4 %all-gather.6.cloned.1.call-done = bf16[4096,1024]{1,0:T(8,128)(2,1)} async-done(((bf16[512,1024]{1,0:T(8,128)(2,1)}), bf16[4096,1024]{1,0:T(8,128)(2,1)}) %all-gather.6.cloned.1.call-update) | async-done | bytes 8388624 | tf_op jit(solution)/shard_map/all_gather | solution.py:47
  560.7 9.1 %fusion.3 = bf16[512,1024]{0,1:T(8,128)(2,1)S(1)} fusion(bf16[4096,1024]{1,0:T(8,128)(2,1)} %all-gather.6.cloned.1.call-done, bf16[512,4096]{1,0:T(8,128)(2,1)} %all-gather.8.cloned.1.call-done), kind=kOutput, calls=%fused_computation.9 | convolution fusion | flops 4295491584 | bytes 13631488 | tf_op jit(solution)/shard_map/dot_general | solution.py:45
  569.8 1.3 copy.11
  (14 shorter events, 0.0 us)
Async XLA Ops:
  7.2 78.9 %copy-start = (bf16[512,1024]{1,0:T(8,128)(2,1)S(1)}, bf16[512,1024]{1,0:T(8,128)(2,1)}, u32[]{:S(2)}) copy-start(bf16[512,1024]{1,0:T(8,128)(2,1)} %param.7) | copy-start | bytes 3145732
  7.2 78.9 %all-gather.4.cloned.1.call-start = ((), (), s32[]{:S(2)}) async-start(), calls=%async_computation.1 | async-start | bytes 4325376 | tf_op jit(solution)/shard_map/all_gather | solution.py:17
  7.9 283.0 %reduce-scatter.2.cloned.1.call-start = ((), (), s32[]{:S(2)}) async-start(), calls=%async_computation.2 | async-start | bytes 18874368 | tf_op jit(solution)/shard_map/reduce_scatter | solution.py:22
  96.5 1.6 copy-start.2
  96.5 355.8 %all-gather.8.cloned.1.call-start = ((), (), s32[]{:S(2)}) async-start(), calls=%async_computation.4 | async-start | bytes 4325376 | tf_op jit(solution)/shard_map/all_gather | solution.py:18
  97.2 271.2 %copy-start.6 = (f32[512]{0:T(512)S(1)}, f32[512]{0:T(512)}, u32[]{:S(2)}) copy-start(f32[512]{0:T(512)} %param.9) | copy-start | bytes 6148
  97.3 271.2 %copy-start.5 = (f32[1024]{0:T(1024)S(1)}, f32[1024]{0:T(1024)}, u32[]{:S(2)}) copy-start(f32[1024]{0:T(1024)} %param.10) | copy-start | bytes 12292
  97.3 463.4 %all-gather.6.cloned.1.call-start = ((), (), s32[]{:S(2)}) async-start(), calls=%async_computation.3 | async-start | bytes 9437184 | tf_op jit(solution)/shard_map/all_gather | solution.py:47
  290.9 77.6 %copy-start.1 = (f32[512,1024]{1,0:T(8,128)S(1)}, f32[512,1024]{1,0:T(8,128)}, u32[]{:S(2)}) copy-start(f32[512,1024]{1,0:T(8,128)} %reduce-scatter.2.cloned.1.call-done) | copy-start | bytes 6291460
  368.5 83.8 %copy-start.4 = (f32[512]{0:T(512)}, f32[512]{0:T(512)S(1)}, u32[]{:S(2)}) copy-start(f32[512]{0:T(512)S(1)} %multiply_add_fusion.2) | copy-start | bytes 6148
  368.5 83.7 %copy-start.3 = (f32[1024]{0:T(1024)}, f32[1024]{0:T(1024)S(1)}, u32[]{:S(2)}) copy-start(f32[1024]{0:T(1024)S(1)} %multiply_add_fusion.1) | copy-start | bytes 12292
Sparse Core Ops, SparseCore 0:
  9.8 76.3 all-gather.3
  96.6 194.2 reduce-scatter.1
  292.7 75.3 all-gather.7
  452.4 108.2 all-gather.5
where the time goes:
time: 578 us
  waiting for transfers between devices  380 us (66%)
  blocking collectives  152 us (26%)
  matrix products  19.5 us (3%)
  between operations  15.2 us (3%)
  other arithmetic  9.27 us (2%)
    reduce_scatter x1, waiting for transfers between devices, body(): lax.psum_scatter(lax.dot_general(block, out_grads, contract, preferred_el...  192 us
    all_gather x1, waiting for transfers between devices, body(): lax.all_gather(weight_half, 'dp', axis=0, tiled=True)  108 us
    all_gather x1, waiting for transfers between devices, body(): lax.all_gather(activations, 'mp', axis=1, tiled=True)  78.1 us
    psum x1, blocking collectives, body(): lax.psum((jnp.sum(raw_update * raw_update), jnp.sum(weight * weight)), ('...  76.3 us
    psum x1, blocking collectives, body(): row_sum = lax.psum(row_part, 'mp')  56.9 us
    psum x1, blocking collectives, body(): column_sum = lax.psum(column_part, 'dp')  18.5 us
  transfers between devices with their start and end apart: 4, of which 3 were waited for; matrix products, arithmetic and copies ran while one was open for 2% of the time, Pallas kernels for 0%

commit v1 on v0

--- a/solution.py
+++ b/solution.py
@@ -10,11 +10,14 @@
 decay_rate = 0.5
 clip_level = 0.5
 learn_rate = 0.01
+move_run = lambda a0, mesh_ax: jnp.concatenate(
+    jax.lax.all_to_all(jnp.stack(jax.lax.axis_size(mesh_ax) * [a0]), mesh_ax, 0, 0), 1
+)
 
 
 def body(activations, out_grads, weight, row_state, column_state, next_batch):
     features, next_features = (
-        lax.all_gather(activations, "mp", axis=1, tiled=True),
+        move_run(activations, mesh_ax="mp"),
         lax.all_gather(next_batch, "mp", axis=1, tiled=True),
     )
     contract = (((0,), (0,)), ((), ()))

time: 578 us -> 617 us (1.067)
  blocking collectives: 152 us -> 257 us
  waiting for transfers between devices: 380 us -> 312 us
    all_to_all x0 -> x1, blocking collectives: none -> 106 us  [jax.lax.all_to_all(jnp.stack(jax.lax.axis_size(mesh_ax) * [a0]), mesh_ax,...]
    all_gather x1 -> x0, waiting for transfers between devices: 78.1 us -> none  [body(): lax.all_gather(activations, 'mp', axis=1, tiled=True)]
    reduce_scatter x1, waiting for transfers between devices: 192 us -> 203 us  [body(): lax.psum_scatter(lax.dot_general(block, out_grads, contract, preferred_el...]
  transfers between devices with their start and end apart: 4 -> 3, of which waited for: 3 -> 2; matrix products, arithmetic and copies ran while one was open for 2% -> 2% of each run, Pallas kernels for 0% -> 0%
where the time goes in v1:
time: 617 us
  waiting for transfers between devices  312 us (51%)
  blocking collectives  257 us (42%)
  matrix products  17.2 us (3%)
  between operations  17 us (3%)
  other arithmetic  9.27 us (2%)
    reduce_scatter x1, waiting for transfers between devices, body(): lax.psum_scatter(lax.dot_general(block, out_grads, contract, preferred_el...  203 us
    all_gather x1, waiting for transfers between devices, body(): lax.all_gather(weight_half, 'dp', axis=0, tiled=True)  109 us
    all_to_all x1, blocking collectives, jax.lax.all_to_all(jnp.stack(jax.lax.axis_size(mesh_ax) * [a0]), mesh_ax,...  106 us
    psum x1, blocking collectives, body(): lax.psum((jnp.sum(raw_update * raw_update), jnp.sum(weight * weight)), ('...  76.1 us
    psum x1, blocking collectives, body(): row_sum = lax.psum(row_part, 'mp')  56.4 us
    psum x1, blocking collectives, body(): column_sum = lax.psum(column_part, 'dp')  18.5 us
  transfers between devices with their start and end apart: 3, of which 2 were waited for; matrix products, arithmetic and copies ran while one was open for 2% of the time, Pallas kernels for 0%

profile of v1, /device:TPU:1, one launch (start us, length us, event | category | flops | bytes accessed | tf_op | source)
XLA Modules:
  0.0 616.8 jit_solution(18198121364845942252)
XLA Ops:
  8.0 0.0 copy-start
  8.0 0.0 reduce-scatter.2.cloned.1.call-start
  8.1 1.1 copy.12
  9.1 0.5 stack.2
  9.6 106.3 %all_to_all.5 = bf16[32,512,128]{1,2,0:T(8,128)(2,1)S(1)} all-to-all(bf16[32,512,128]{1,2,0:T(8,128)(2,1)S(1)} %stack.2), channel_id=1, replica_groups=mesh['dp'=8,'mp'=32] {'mp'}, dimensions={0} | all-to-all | bytes 8388608 | tf_op jit(solution)/shard_map/all_to_all | solution.py:14
  115.9 8.1 %fusion.6 = f32[4096,1024]{1,0:T(8,128)} fusion(bf16[512,4096]{0,1:T(8,128)(2,1)S(1)} %bitcast.9, bf16[512,1024]{1,0:T(8,128)(2,1)S(1)} %copy-done), kind=kOutput, calls=%fused_computation.13 | convolution fusion | flops 4294967296 | bytes 22020096 | tf_op jit(solution)/shard_map/dot_general | solution.py:26
  124.0 0.0 reduce-scatter.2.cloned.1.call-update
  124.0 0.0 all-gather.5.cloned.1.call-start
  124.1 0.5 all-gather.5.cloned.1.call-update
  124.6 0.0 all-gather.3.cloned.1.call-start
  124.7 0.9 copy-done.2
  125.6 1.1 multiply_reduce_fusion.1
  126.7 202.8 %reduce-scatter.2.cloned.1.call-done = f32[512,1024]{1,0:T(8,128)} async-done(((f32[4096,1024]{1,0:T(8,128)}), f32[512,1024]{1,0:T(8,128)}) %reduce-scatter.2.cloned.1.call-update) | async-done | bytes 2097168 | tf_op jit(solution)/shard_map/reduce_scatter | solution.py:25
  329.5 2.1 fusion.1
  331.7 56.4 %psum.29 = f32[512]{0:T(512)S(1)} all-reduce(f32[512]{0:T(512)S(1)} %get-tuple-element.15), channel_id=1, replica_groups=mesh['dp'=8,'mp'=32] {'mp'}, use_global_device_ids=true, to_apply=%region_4.0 | all-reduce | flops 512 | bytes 4096 | tf_op jit(solution)/shard_map/psum | solution.py:34
  388.1 18.5 %psum.30 = f32[1024]{0:T(1024)S(1)} all-reduce(f32[1024]{0:T(1024)S(1)} %get-tuple-element.16), channel_id=1, replica_groups=mesh['dp'=8,'mp'=32] {'dp'}, use_global_device_ids=true, to_apply=%region_6.0 | all-reduce | flops 1024 | bytes 8192 | tf_op jit(solution)/shard_map/psum | solution.py:35
  406.6 1.5 multiply_reduce_fusion
  408.1 76.1 %all-reduce = (f32[]{:T(128)}, f32[]{:T(128)}) all-reduce(f32[]{:T(128)} %multiply_reduce_fusion, f32[]{:T(128)} %multiply_reduce_fusion.1), channel_id=1, replica_groups=mesh['dp'=8,'mp'=32] {'dp','mp'}, use_global_device_ids=true, to_apply=%region_8.0 | all-reduce | flops 2 | bytes 16 | tf_op jit(solution)/shard_map/psum | solution.py:39
  485.6 4.5 fusion.4
  490.1 0.0 all-gather.3.cloned.1.call-update
  490.1 0.0 all-gather.5.cloned.1.call-done
  490.2 108.8 %all-gather.3.cloned.1.call-done = bf16[4096,1024]{1,0:T(8,128)(2,1)} async-done(((bf16[512,1024]{1,0:T(8,128)(2,1)}), bf16[4096,1024]{1,0:T(8,128)(2,1)}) %all-gather.3.cloned.1.call-update) | async-done | bytes 8388624 | tf_op jit(solution)/shard_map/all_gather | solution.py:50
  599.0 9.1 %fusion.3 = bf16[512,1024]{0,1:T(8,128)(2,1)S(1)} fusion(bf16[4096,1024]{1,0:T(8,128)(2,1)} %all-gather.3.cloned.1.call-done, bf16[512,4096]{1,0:T(8,128)(2,1)} %all-gather.5.cloned.1.call-done), kind=kOutput, calls=%fused_computation.9 | convolution fusion | flops 4295491584 | bytes 13631488 | tf_op jit(solution)/shard_map/dot_general | solution.py:48
  608.1 1.3 copy.13
  (14 shorter events, 0.0 us)
Async XLA Ops:
  8.0 107.9 %copy-start = (bf16[512,1024]{1,0:T(8,128)(2,1)S(1)}, bf16[512,1024]{1,0:T(8,128)(2,1)}, u32[]{:S(2)}) copy-start(bf16[512,1024]{1,0:T(8,128)(2,1)} %param.7) | copy-start | bytes 3145732
  8.0 321.5 %reduce-scatter.2.cloned.1.call-start = ((), (), s32[]{:S(2)}) async-start(), calls=%async_computation.2 | async-start | bytes 18874368 | tf_op jit(solution)/shard_map/reduce_scatter | solution.py:25
  124.0 1.6 copy-start.2
  124.0 366.1 %all-gather.5.cloned.1.call-start = ((), (), s32[]{:S(2)}) async-start(), calls=%async_computation.4 | async-start | bytes 4325376 | tf_op jit(solution)/shard_map/all_gather | solution.py:21
  124.6 282.0 %copy-start.6 = (f32[512]{0:T(512)S(1)}, f32[512]{0:T(512)}, u32[]{:S(2)}) copy-start(f32[512]{0:T(512)} %param.9) | copy-start | bytes 6148
  124.6 282.0 %copy-start.5 = (f32[1024]{0:T(1024)S(1)}, f32[1024]{0:T(1024)}, u32[]{:S(2)}) copy-start(f32[1024]{0:T(1024)} %param.10) | copy-start | bytes 12292
  124.6 474.4 %all-gather.3.cloned.1.call-start = ((), (), s32[]{:S(2)}) async-start(), calls=%async_computation.3 | async-start | bytes 9437184 | tf_op jit(solution)/shard_map/all_gather | solution.py:50
  329.5 77.1 %copy-start.1 = (f32[512,1024]{1,0:T(8,128)S(1)}, f32[512,1024]{1,0:T(8,128)}, u32[]{:S(2)}) copy-start(f32[512,1024]{1,0:T(8,128)} %reduce-scatter.2.cloned.1.call-done) | copy-start | bytes 6291460
  406.6 83.5 %copy-start.4 = (f32[512]{0:T(512)}, f32[512]{0:T(512)S(1)}, u32[]{:S(2)}) copy-start(f32[512]{0:T(512)S(1)} %multiply_add_fusion.2) | copy-start | bytes 6148
  406.6 83.5 %copy-start.3 = (f32[1024]{0:T(1024)}, f32[1024]{0:T(1024)S(1)}, u32[]{:S(2)}) copy-start(f32[1024]{0:T(1024)S(1)} %multiply_add_fusion.1) | copy-start | bytes 12292
Sparse Core Ops, SparseCore 0:
  124.1 205.3 reduce-scatter.1
Sparse Core Ops, SparseCore 1:
  126.3 83.1 all-gather.4
  490.2 108.7 all-gather.2

commit v2 on v0

--- a/solution.py
+++ b/solution.py
@@ -10,6 +10,12 @@
 decay_rate = 0.5
 clip_level = 0.5
 learn_rate = 0.01
+
+
+def summed_here(shard, axis):
+    parts = lax.all_gather(shard, axis, axis=0, tiled=False)
+    result = parts.sum(axis=0)
+    return result
 
 
 def body(activations, out_grads, weight, row_state, column_state, next_batch):
@@ -28,7 +34,7 @@
     squares = gradient * gradient + tiny_square
     row_part = jnp.sum(squares, axis=1)
     column_part = jnp.sum(squares, axis=0)
-    row_sum = lax.psum(row_part, "mp")
+    row_sum = summed_here(row_part, "mp")
     column_sum = lax.psum(column_part, "dp")
     row_moment = decay_rate * row_state + (1.0 - decay_rate) * (row_sum / FF)
     column_moment = decay_rate * column_state + (1.0 - decay_rate) * (column_sum / D)

time: 578 us -> 557 us (0.964)
  blocking collectives: 152 us -> 131 us
    psum x1 -> x0, blocking collectives: 56.9 us -> none  [body(): row_sum = lax.psum(row_part, 'mp')]
    all_gather x0 -> x1, blocking collectives: none -> 38.2 us  [summed_here(): parts = lax.all_gather(shard, axis, axis=0, tiled=False)]
where the time goes in v2:
time: 557 us
  waiting for transfers between devices  379 us (68%)
  blocking collectives  131 us (24%)
  matrix products  19.5 us (4%)
  between operations  15.2 us (3%)
  other arithmetic  9.33 us (2%)
    reduce_scatter x1, waiting for transfers between devices, body(): lax.psum_scatter(lax.dot_general(block, out_grads, contract, preferred_el...  192 us
    all_gather x1, waiting for transfers between devices, body(): lax.all_gather(weight_half, 'dp', axis=0, tiled=True)  108 us
    all_gather x1, waiting for transfers between devices, body(): lax.all_gather(activations, 'mp', axis=1, tiled=True)  78.1 us
    psum x1, blocking collectives, body(): lax.psum((jnp.sum(raw_update * raw_update), jnp.sum(weight * weight)), ('...  74.3 us
    all_gather x1, blocking collectives, summed_here(): parts = lax.all_gather(shard, axis, axis=0, tiled=False)  38.2 us
    psum x1, blocking collectives, body(): column_sum = lax.psum(column_part, 'dp')  18.6 us
  transfers between devices with their start and end apart: 4, of which 3 were waited for; matrix products, arithmetic and copies ran while one was open for 2% of the time, Pallas kernels for 0%

profile of v2, /device:TPU:1, one launch (start us, length us, event | category | flops | bytes accessed | tf_op | source)
XLA Modules:
  0.0 556.8 jit_solution(1035655176002972448)
XLA Ops:
  7.2 0.0 all-gather.6.cloned.1.call-start
  7.2 0.7 all-gather.6.cloned.1.call-update
  7.9 0.0 reduce-scatter.2.cloned.1.call-start
  8.0 78.1 %all-gather.6.cloned.1.call-done = bf16[512,4096]{1,0:T(8,128)(2,1)} async-done(((bf16[512,128]{1,0:T(8,128)(2,1)}), bf16[512,4096]{1,0:T(8,128)(2,1)}) %all-gather.6.cloned.1.call-update) | async-done | bytes 4194320 | tf_op jit(solution)/shard_map/all_gather | solution.py:23
  86.1 10.4 %fusion.6 = f32[4096,1024]{1,0:T(8,128)} fusion(bf16[512,4096]{1,0:T(8,128)(2,1)} %all-gather.6.cloned.1.call-done, bf16[512,1024]{1,0:T(8,128)(2,1)S(1)} %copy-done), kind=kOutput, calls=%fused_computation.13 | convolution fusion | flops 4294967296 | bytes 22020096 | tf_op jit(solution)/shard_map/dot_general | solution.py:29
  96.5 0.0 reduce-scatter.2.cloned.1.call-update
  96.5 0.0 all-gather.10.cloned.1.call-start
  96.5 0.7 all-gather.10.cloned.1.call-update
  97.3 0.0 all-gather.8.cloned.1.call-start
  97.3 0.8 copy-done.2
  98.1 1.1 multiply_reduce_fusion.1
  99.2 191.7 %reduce-scatter.2.cloned.1.call-done = f32[512,1024]{1,0:T(8,128)} async-done(((f32[4096,1024]{1,0:T(8,128)}), f32[512,1024]{1,0:T(8,128)}) %reduce-scatter.2.cloned.1.call-update) | async-done | bytes 2097168 | tf_op jit(solution)/shard_map/reduce_scatter | solution.py:28
  290.9 2.1 fusion.1
  293.1 38.2 %all-gather.1 = f32[32,1,512]{2,1,0:T(1,128)S(1)} all-gather(f32[1,1,512]{2,1,0:T(1,128)S(1)} %bitcast.7), channel_id=2, replica_groups=mesh['dp'=8,'mp'=32] {'mp'}, dimensions={0}, use_global_device_ids=true | all-gather | bytes 67584 | tf_op jit(solution)/shard_map/all_gather | solution.py:16
  331.3 0.1 reduce_sum.47
  331.4 18.6 %psum.22 = f32[1024]{0:T(1024)S(1)} all-reduce(f32[1024]{0:T(1024)S(1)} %get-tuple-element.16), channel_id=1, replica_groups=mesh['dp'=8,'mp'=32] {'dp'}, use_global_device_ids=true, to_apply=%region_6.0 | all-reduce | flops 1024 | bytes 8192 | tf_op jit(solution)/shard_map/psum | solution.py:38
  350.1 1.5 multiply_reduce_fusion
  351.6 74.3 %all-reduce = (f32[]{:T(128)}, f32[]{:T(128)}) all-reduce(f32[]{:T(128)} %multiply_reduce_fusion, f32[]{:T(128)} %multiply_reduce_fusion.1), channel_id=1, replica_groups=mesh['dp'=8,'mp'=32] {'dp','mp'}, use_global_device_ids=true, to_apply=%region_8.0 | all-reduce | flops 2 | bytes 16 | tf_op jit(solution)/shard_map/psum | solution.py:42
  427.3 4.5 fusion.4
  431.8 0.0 all-gather.8.cloned.1.call-update
  431.8 0.0 all-gather.10.cloned.1.call-done
  431.8 108.0 %all-gather.8.cloned.1.call-done = bf16[4096,1024]{1,0:T(8,128)(2,1)} async-done(((bf16[512,1024]{1,0:T(8,128)(2,1)}), bf16[4096,1024]{1,0:T(8,128)(2,1)}) %all-gather.8.cloned.1.call-update) | async-done | bytes 8388624 | tf_op jit(solution)/shard_map/all_gather | solution.py:53
  539.8 9.1 %fusion.3 = bf16[512,1024]{0,1:T(8,128)(2,1)S(1)} fusion(bf16[4096,1024]{1,0:T(8,128)(2,1)} %all-gather.8.cloned.1.call-done, bf16[512,4096]{1,0:T(8,128)(2,1)} %all-gather.10.cloned.1.call-done), kind=kOutput, calls=%fused_computation.9 | convolution fusion | flops 4295491584 | bytes 13631488 | tf_op jit(solution)/shard_map/dot_general | solution.py:51
  548.9 1.3 copy.12
  (15 shorter events, 0.1 us)
Async XLA Ops:
  7.2 78.9 %copy-start = (bf16[512,1024]{1,0:T(8,128)(2,1)S(1)}, bf16[512,1024]{1,0:T(8,128)(2,1)}, u32[]{:S(2)}) copy-start(bf16[512,1024]{1,0:T(8,128)(2,1)} %param.7) | copy-start | bytes 3145732
  7.2 78.9 %all-gather.6.cloned.1.call-start = ((), (), s32[]{:S(2)}) async-start(), calls=%async_computation.1 | async-start | bytes 4325376 | tf_op jit(solution)/shard_map/all_gather | solution.py:23
  7.9 283.0 %reduce-scatter.2.cloned.1.call-start = ((), (), s32[]{:S(2)}) async-start(), calls=%async_computation.2 | async-start | bytes 18874368 | tf_op jit(solution)/shard_map/reduce_scatter | solution.py:28
  96.5 1.6 copy-start.2
  96.5 335.3 %all-gather.10.cloned.1.call-start = ((), (), s32[]{:S(2)}) async-start(), calls=%async_computation.4 | async-start | bytes 4325376 | tf_op jit(solution)/shard_map/all_gather | solution.py:24
  97.2 252.8 %copy-start.6 = (f32[512]{0:T(512)S(1)}, f32[512]{0:T(512)}, u32[]{:S(2)}) copy-start(f32[512]{0:T(512)} %param.9) | copy-start | bytes 6148
  97.3 252.8 %copy-start.5 = (f32[1024]{0:T(1024)S(1)}, f32[1024]{0:T(1024)}, u32[]{:S(2)}) copy-start(f32[1024]{0:T(1024)} %param.10) | copy-start | bytes 12292
  97.3 442.5 %all-gather.8.cloned.1.call-start = ((), (), s32[]{:S(2)}) async-start(), calls=%async_computation.3 | async-start | bytes 9437184 | tf_op jit(solution)/shard_map/all_gather | solution.py:53
  290.9 59.2 %copy-start.1 = (f32[512,1024]{1,0:T(8,128)S(1)}, f32[512,1024]{1,0:T(8,128)}, u32[]{:S(2)}) copy-start(f32[512,1024]{1,0:T(8,128)} %reduce-scatter.2.cloned.1.call-done) | copy-start | bytes 6291460
  350.0 81.7 %copy-start.4 = (f32[512]{0:T(512)}, f32[512]{0:T(512)S(1)}, u32[]{:S(2)}) copy-start(f32[512]{0:T(512)S(1)} %multiply_add_fusion.2) | copy-start | bytes 6148
  350.1 81.7 %copy-start.3 = (f32[1024]{0:T(1024)}, f32[1024]{0:T(1024)S(1)}, u32[]{:S(2)}) copy-start(f32[1024]{0:T(1024)S(1)} %multiply_add_fusion.1) | copy-start | bytes 12292
Sparse Core Ops, SparseCore 0:
  9.8 76.3 all-gather.5
  96.6 194.2 reduce-scatter.1
  292.7 75.2 all-gather.9
  431.9 107.8 all-gather.7
